TPU v7x, 128 devices: a whole 4x4x4 slice. The times are simulated.
128 devices in a mesh: gx: 16 (over z, y_lo, core), gy: 8 (over x, y_hi).
Axes of the slice: x: 4, y: 4 (y_hi: 2, y_lo: 2; y = y_hi * 2 + y_lo), z: 4, core: 2. Of those that a mesh axis runs over, the one named last changes fastest.
Arguments:
- velocity: float32 [3, 4096, 1024], P(None, 'gx', 'gy'), may hold values from 0.4 to 1.6
- adjoint_seed: float32 [3, 4096, 1024], P(None, 'gx', 'gy'), may hold values from -6 to 6
- courant: float32 [3, 4096, 1024], P(None, 'gx', 'gy'), may hold values from 0.1 to 0.45
- viscosity: float32 [3, 4096, 1024], P(None, 'gx', 'gy'), may hold values from 0.02 to 0.1
- turbine_tile: int32 [512, 1], P(('gx', 'gy')), may hold values from 0 to 127; in each aligned block of 512 rows (0 to 511, 512 to 1023, ...) at most 12 rows name the same one
- turbine_offset: int32 [512, 2], P(('gx', 'gy')), may hold values from 0 to 64
- thrust: float32 [512], P(('gx', 'gy')), may hold values from 0.5 to 2
- disk_width: float32 [512], P(('gx', 'gy')), may hold values from 8 to 16
Outputs:
- adjoint_start: float32 [3, 4096, 1024], P(None, 'gx', 'gy')
- thrust_grad: float32 [512], P(('gx', 'gy'))
Inputs may be any that keep to these rules, and one draw needn't show every extreme that they name: `turbine_tile`: each turbine's tile is the index along gx times the number of devices of gy plus the index along gy of the device whose cells hold its footprint. No tile holds more than 12 turbines, and some tile holds exactly 12.
All inputs are finite; a program needn't handle non-finite values.
Results may differ from a plain program's by a relative error of at most 0.00002.
Values sent between devices are 32-bit elements; how exact they have to be, the bound alone decides.
A program may use at most 128 MiB of HBM per device.

v0:
```python
import jax
import jax.numpy as jnp
from jax import lax
from jax.sharding import PartitionSpec as P

LEV = 3
STEPS = 8
FP = 64
VERTICAL_MIX = 0.05
DRAG_SCALE = 0.01


def padded_2(block, sides, width):
    for axis, dim in sides:
        count = lax.axis_size(axis)
        forward = [(i, i + 1) for i in range(count - 1)]
        forward.append((count - 1, 0))
        backward = [(target, source) for source, target in forward]
        low = lax.ppermute(
            lax.slice_in_dim(block, block.shape[dim] - width, None, axis=dim), axis, forward
        )
        high = lax.ppermute(lax.slice_in_dim(block, 0, width, axis=dim), axis, backward)
        block = jnp.concatenate([low, block, high], axis=dim)
    return block


def drag_law(state):
    return state * jnp.sqrt(state * state + 1.0)


def drag_slope(state):
    square_one = state * state + 1.0
    return (square_one + state * state) / jnp.sqrt(square_one)


def vertical(center):
    zero_row = jnp.zeros_like(center[:1])
    from_above = jnp.concatenate([center[1:] - center[:-1], zero_row], axis=0)
    from_below = jnp.concatenate([zero_row, center[:-1] - center[1:]], axis=0)
    return from_above + from_below


def advance(padded, advect, diffuse, drag_coef):
    center = padded[:, 1:-1, 1:-1]
    upwind = padded[:, :-2, 1:-1]
    downwind = padded[:, 2:, 1:-1]
    left_cell = padded[:, 1:-1, :-2]
    right_cell = padded[:, 1:-1, 2:]
    return (
        center
        + advect * (upwind - center)
        + diffuse * (downwind + upwind + right_cell + left_cell - 4.0 * center)
        + VERTICAL_MIX * vertical(center)
        - drag_coef * drag_law(center)
    )


def retreat(padded, advect_ext, diffuse_ext, drag_coef, state):
    flux_adv = advect_ext * padded
    flux_dif = diffuse_ext * padded
    center = padded[:, 1:-1, 1:-1]
    return (
        center
        - flux_adv[:, 1:-1, 1:-1]
        - 4.0 * flux_dif[:, 1:-1, 1:-1]
        + flux_adv[:, 2:, 1:-1]
        + (
            flux_dif[:, 2:, 1:-1]
            + flux_dif[:, :-2, 1:-1]
            + flux_dif[:, 1:-1, 2:]
            + flux_dif[:, 1:-1, :-2]
        )
        + VERTICAL_MIX * vertical(center)
        - drag_coef * drag_slope(state) * center
    )


def footprint(disk_width):
    cell_pos = jnp.arange(FP, dtype=jnp.float32) - (FP - 1) / 2.0
    profile = jnp.exp(
        -(cell_pos[None, :] * cell_pos[None, :]) / (2.0 * disk_width[:, None] * disk_width[:, None])
    )
    level_pos = jnp.arange(LEV, dtype=jnp.float32) - (LEV - 1) / 2.0
    level_gain = DRAG_SCALE * jnp.exp(-0.5 * level_pos * level_pos)
    return level_gain[None, :, None, None] * profile[:, None, :, None] * profile[:, None, None, :]


def extend_rim(array, rim_depth):
    return padded_2(array, (("gx", 1), ("gy", 2)), rim_depth)


def trim_rim(array, stored_margin, wanted):
    excess = stored_margin - wanted
    if excess == 0:
        return array
    return array[:, excess:-excess, excess:-excess]


def coef_at(coef_ext, coef_margin, wanted, levels):
    portion = trim_rim(coef_ext, coef_margin, wanted)
    return (portion[:levels], portion[levels : 2 * levels], portion[2 * levels : 3 * levels])


def shards(
    velocity, adjoint_seed, courant, viscosity, turbine_tile, turbine_offset, thrust, disk_width
):
    levels = velocity.shape[0]
    places, shifts = (
        lax.all_gather(turbine_tile, ("gx", "gy"), axis=0, tiled=True),
        lax.all_gather(turbine_offset, ("gx", "gy"), axis=0, tiled=True),
    )
    thrusts, widths = (
        lax.all_gather(thrust, ("gx", "gy"), axis=0, tiled=True),
        lax.all_gather(disk_width, ("gx", "gy"), axis=0, tiled=True),
    )
    turbine_count = places.shape[0]
    own_index = lax.axis_index("gx") * lax.axis_size("gy") + lax.axis_index("gy")
    turbine_ids = jnp.arange(turbine_count, dtype=jnp.int32)
    in_tile = places[:, 0] == own_index
    sort_keys = jnp.where(in_tile, turbine_ids, turbine_ids + turbine_count)
    slot_count = 3 * thrust.shape[0]
    slot_ids = jnp.argsort(sort_keys)[:slot_count]
    slot_match = in_tile[slot_ids]
    slot_live = slot_match.astype(jnp.float32)
    slot_rows = shifts[slot_ids, 0]
    slot_cols = shifts[slot_ids, 1]
    kernels = footprint(widths[slot_ids])
    slot_thrust = thrusts[slot_ids] * slot_live

    def add_turbine(slot_index, field_now):
        corner = (jnp.int32(0), slot_rows[slot_index], slot_cols[slot_index])
        block_vals = lax.dynamic_slice(field_now, corner, (levels, FP, FP))
        return lax.dynamic_update_slice(
            field_now, block_vals + slot_thrust[slot_index] * kernels[slot_index], corner
        )

    drag_field = lax.fori_loop(0, slot_count, add_turbine, jnp.zeros_like(velocity))
    forward_depth = 1
    coef_margin = 1
    coef_margin = forward_depth
    coef_ext = extend_rim(jnp.concatenate([courant, viscosity, drag_field], axis=0), forward_depth)
    state = velocity
    state_margin = 0
    states = []
    for step_index in range(STEPS):
        if step_index + 1 < STEPS and state_margin == 0:
            state = extend_rim(state, forward_depth)
            state_margin = forward_depth
        states.append((state, state_margin))
        if step_index + 1 < STEPS:
            advect, diffuse, drag_coef = coef_at(coef_ext, coef_margin, state_margin - 1, levels)
            state = advance(state, advect, diffuse, drag_coef)
            state_margin = state_margin - 1
    adjoint = adjoint_seed
    adjoint_margin = 0
    sensitivity = jnp.zeros_like(velocity)
    for step_index in reversed(range(STEPS)):
        stored, stored_margin = states[step_index]
        sensitivity = sensitivity - trim_rim(adjoint, adjoint_margin, 0) * drag_law(
            trim_rim(stored, stored_margin, 0)
        )
        adjoint = extend_rim(adjoint, forward_depth)
        adjoint_margin = forward_depth
        advect_ext, diffuse_ext, unused_drag = coef_at(
            coef_ext, coef_margin, adjoint_margin, levels
        )
        unused_adv, unused_dif, drag_mid = coef_at(
            coef_ext, coef_margin, adjoint_margin - 1, levels
        )
        adjoint = retreat(
            adjoint,
            advect_ext,
            diffuse_ext,
            drag_mid,
            trim_rim(stored, stored_margin, adjoint_margin - 1),
        )
        adjoint_margin = adjoint_margin - 1
    adjoint_start = trim_rim(adjoint, adjoint_margin, 0)

    def slot_total(row_first, col_first, kernel):
        block_vals = lax.dynamic_slice(
            sensitivity, (jnp.int32(0), row_first, col_first), (levels, FP, FP)
        )
        return jnp.sum(kernel * block_vals)

    totals = jax.vmap(slot_total)(slot_rows, slot_cols, kernels)
    values = thrusts[slot_ids] * totals * slot_live
    one_hot = (turbine_ids[None, :] == slot_ids[:, None]).astype(jnp.float32)
    spread = jnp.sum(one_hot * values[:, None], axis=0)
    return (adjoint_start, lax.psum_scatter(spread, ("gx", "gy"), scatter_dimension=0, tiled=True))


def solution(mesh):
    placed = (
        P(None, "gx", "gy"),
        P(None, "gx", "gy"),
        P(None, "gx", "gy"),
        P(None, "gx", "gy"),
        P(("gx", "gy"), None),
        P(("gx", "gy"), None),
        P(("gx", "gy")),
        P(("gx", "gy")),
    )
    return jax.shard_map(
        shards,
        mesh=mesh,
        in_specs=placed,
        out_specs=(P(None, "gx", "gy"), P(("gx", "gy"))),
        check_vma=False,
    )
```

profile of v0, /device:TPU:1, one launch (start us, length us, event | category | flops | bytes accessed | tf_op | source)
XLA Modules:
  0.0 1061.2 jit_solution(10426289407377339527)
XLA Ops:
  6.1 69.8 %all-reduce.32 = s32[512]{0:T(512)S(1)} all-reduce(s32[512]{0:T(512)S(1)} %bitcast_dynamic-update-slice_fusion.1), channel_id=1, replica_groups=mesh['gx'=16,'gy'=8] {'gx','gy'}, use_global_device_ids=true, to_apply=%add.32 | all-reduce | flops 512 | bytes 4096
  75.9 3.8 sort.17
  80.3 303.1 %all-gather = s32[128,4,2]{1,2,0:T(2,128)S(1)} all-gather(s32[1,4,2]{1,2,0:T(2,128)} %bitcast.32), channel_id=1, replica_groups=mesh['gx'=16,'gy'=8] {'gx','gy'}, dimensions={0}, use_global_device_ids=true | all-gather | bytes 4128 | tf_op jit(solution)/shard_map/all_gather | solution.py:110
  386.2 71.6 %all-reduce.36 = (f32[512]{0:T(512)S(1)}, f32[512]{0:T(512)S(1)}) all-reduce(f32[512]{0:T(512)S(1)} %dynamic-update-slice.3, f32[512]{0:T(512)S(1)} %dynamic-update-slice.4), channel_id=1, replica_groups=mesh['gx'=16,'gy'=8] {'gx','gy'}, use_global_device_ids=true, to_apply=%add.33 | all-reduce | flops 1024 | bytes 8192
  460.0 99.8 %while.14 = (s32[]{:T(128)}, f32[3,256,128]{2,1,0:T(8,128)S(1)}, s32[12]{0:T(128)S(1)}, s32[12]{0:T(128)S(1)}, f32[12]{0:T(128)S(1)}, /*index=5*/f32[12,3,64,64]...) while((s32[]{:T(128)}, f32[3,256,128]{2,1,0:T(8,128)S(1)}, s32[12]{0:T(128)S(1)}, ...), condition=%wide.region_2.3_spmd, body=%wide.region_1.2_spmd.sunk | while | flops 24584 | bytes 245993 | solution.py:137
  578.1 4.5 collective-permute-start.14
  584.9 6.0 fusion.113
  591.0 4.8 collective-permute-start.17
  602.0 5.0 collective-permute-start.18
  609.3 5.9 fusion.102
  632.9 5.9 fusion.91
  638.9 5.9 collective-permute-start.25
  645.2 4.7 collective-permute-start.7
  653.1 5.1 collective-permute-start.26
  660.6 6.0 fusion.80
  674.3 5.0 collective-permute-start.30
  682.3 5.0 fusion.69
  699.8 3.9 collective-permute-start.34
  725.1 5.1 fusion.131
  730.4 4.9 fusion.130
  735.4 4.1 fusion.121
  739.6 5.7 collective-permute-start.37
  751.4 4.7 collective-permute-start.39
  770.8 6.0 collective-permute-start.41
  798.2 5.3 collective-permute-start.45
  825.1 5.3 collective-permute-start.49
  852.0 5.3 collective-permute-start.53
  880.4 5.3 collective-permute-start.57
  906.6 9.2 multiply_subtract_fusion
  916.8 5.4 collective-permute-start.61
  923.2 49.5 %while.15 = (s32[]{:T(128)}, f32[3,256,128]{2,1,0:T(8,128)}, s32[12,3]{0,1:T(4,128)}, f32[12,3,64,64]{3,2,1,0:T(8,128)}, s32[]{:T(128)}) while((s32[]{:T(128)}, f32[3,256,128]{2,1,0:T(8,128)}, s32[12,3]{0,1:T(4,128)}, f32[12,3,64,64]{3,2,1,0:T(8,128)}, s32[]{:T(128)}) %tuple.129), condition=%wide.while_cond, body=%wide.while_body.sunk | while | flops 2 | bytes 197749 | solution.py:181
  985.3 65.9 %all-reduce.35 = f32[512]{0:T(512)} all-reduce(f32[512]{0:T(512)} %select_reduce_fusion), channel_id=2, replica_groups=mesh['gx'=16,'gy'=8] {'gx','gy'}, use_global_device_ids=true, to_apply=%region_5.6.clone | all-reduce | flops 512 | bytes 4096
  (602 shorter events, 363.2 us)
Async XLA Ops:
  1.4 559.4 %collective-permute-start.9 = (f32[3,1,128]{2,1,0:T(1,128)S(1)}, f32[3,1,128]{2,1,0:T(1,128)S(1)}, u32[]{:S(2)}, u32[]{:S(2)}) collective-permute-start(f32[3,1,128]{2,1,0:T(1,128)S(1)} %get-tuple-element.326), channel_id=1, source_target_pairs={{8,0},{16,8},{24,16},{32,24},{40,32},{48,40},{56,48},{64,56},{72,6... | collective-permute-start | bytes 4616 | tf_op jit(solution)/shard_map/ppermute | solution.py:22
  2.8 558.0 %collective-permute-start.8 = (f32[3,1,128]{2,1,0:T(1,128)S(1)}, f32[3,1,128]{2,1,0:T(1,128)S(1)}, u32[]{:S(2)}, u32[]{:S(2)}) collective-permute-start(f32[3,1,128]{2,1,0:T(1,128)S(1)} %get-tuple-element.327), channel_id=1, source_target_pairs={{0,8},{8,16},{16,24},{24,32},{32,40},{40,48},{48,56},{56,64},{64,7... | collective-permute-start | bytes 4616 | tf_op jit(solution)/shard_map/ppermute | solution.py:19
  576.9 6.6 collective-permute-start.15
  591.0 7.7 collective-permute-start.17
  595.8 22.9 %collective-permute-start.5 = (f32[3,1,128]{2,1,0:T(1,128)S(1)}, f32[3,1,128]{2,1,0:T(1,128)S(1)}, u32[]{:S(2)}, u32[]{:S(2)}) collective-permute-start(f32[3,1,128]{2,1,0:T(1,128)S(1)} %get-tuple-element.329), channel_id=1, source_target_pairs={{8,0},{16,8},{24,16},{32,24},{40,32},{48,40},{56,48},{64,56},{72,6... | collective-permute-start | bytes 4616 | tf_op jit(solution)/shard_map/ppermute | solution.py:22
  596.4 22.9 %collective-permute-start.4 = (f32[3,1,128]{2,1,0:T(1,128)S(1)}, f32[3,1,128]{2,1,0:T(1,128)}, u32[]{:S(2)}, u32[]{:S(2)}) collective-permute-start(f32[3,1,128]{2,1,0:T(1,128)S(1)} %get-tuple-element.328), channel_id=1, source_target_pairs={{0,8},{8,16},{16,24},{24,32},{32,40},{40,48},{48,56},{56,64},{64,7... | collective-permute-start | bytes 4616 | tf_op jit(solution)/shard_map/ppermute | solution.py:19
  601.3 6.6 collective-permute-start.19
  624.7 6.7 collective-permute-start.23
  638.9 11.3 %collective-permute-start.25 = (f32[3,1,128]{2,0,1:T(4,128)S(1)}, f32[3,1,128]{2,0,1:T(4,128)S(1)}, u32[]{:S(2)}, u32[]{:S(2)}) collective-permute-start(f32[3,1,128]{2,0,1:T(4,128)S(1)} %get-tuple-element.299), channel_id=1, source_target_pairs={{8,0},{16,8},{24,16},{32,24},{40,32},{48,40},{56,48},{64,56},{72,6... | collective-permute-start | bytes 4616 | tf_op jit(solution)/shard_map/ppermute | solution.py:22
  645.2 25.3 %collective-permute-start.7 = (f32[3,258,1]{1,0,2:T(4,128)S(1)}, f32[3,258,1]{1,0,2:T(4,128)S(1)}, u32[]{:S(2)}, u32[]{:S(2)}) collective-permute-start(f32[3,258,1]{1,0,2:T(4,128)S(1)} %copy.743), channel_id=1, source_target_pairs={{1,0},{2,1},{3,2},{4,3},{5,4},{6,5},{7,6},{0,7},{9,8},{10,9},{11,1... | collective-permute-start | bytes 9296 | tf_op jit(solution)/shard_map/ppermute | solution.py:22
  650.1 21.5 %collective-permute-start.6 = (f32[3,258,1]{1,0,2:T(4,128)S(1)}, f32[3,258,1]{1,0,2:T(4,128)S(1)}, u32[]{:S(2)}, u32[]{:S(2)}) collective-permute-start(f32[3,258,1]{1,0,2:T(4,128)S(1)} %copy.742), channel_id=1, source_target_pairs={{0,1},{1,2},{2,3},{3,4},{4,5},{5,6},{6,7},{7,0},{8,9},{9,10},{10,1... | collective-permute-start | bytes 9296 | tf_op jit(solution)/shard_map/ppermute | solution.py:19
  673.5 6.6 collective-permute-start.31
  674.3 7.0 collective-permute-start.30
  690.7 12.9 %collective-permute-start.1 = (f32[9,1,128]{2,0,1:T(8,128)S(1)}, f32[9,1,128]{2,0,1:T(8,128)S(1)}, u32[]{:S(2)}, u32[]{:S(2)}) collective-permute-start(f32[9,1,128]{2,0,1:T(8,128)S(1)} %get-tuple-element.233), channel_id=1, source_target_pairs={{8,0},{16,8},{24,16},{32,24},{40,32},{48,40},{56,48},{64,56},{72,6... | collective-permute-start | bytes 13832 | tf_op jit(solution)/shard_map/ppermute | solution.py:22
  692.7 11.0 %collective-permute-start = (f32[9,1,128]{2,0,1:T(8,128)S(1)}, f32[9,1,128]{2,0,1:T(8,128)S(1)}, u32[]{:S(2)}, u32[]{:S(2)}) collective-permute-start(f32[9,1,128]{2,0,1:T(8,128)S(1)} %get-tuple-element.232), channel_id=1, source_target_pairs={{0,8},{8,16},{16,24},{24,32},{32,40},{40,48},{48,56},{56,64},{64,7... | collective-permute-start | bytes 13832 | tf_op jit(solution)/shard_map/ppermute | solution.py:19
  696.6 19.7 %collective-permute-start.35 = (f32[3,258,1]{1,0,2:T(4,128)S(1)}, f32[3,258,1]{1,0,2:T(4,128)}, u32[]{:S(2)}, u32[]{:S(2)}) collective-permute-start(f32[3,258,1]{1,0,2:T(4,128)S(1)} %copy.698), channel_id=1, source_target_pairs={{0,1},{1,2},{2,3},{3,4},{4,5},{5,6},{6,7},{7,0},{8,9},{9,10},{10,1... | collective-permute-start | bytes 9296 | tf_op jit(solution)/shard_map/ppermute | solution.py:19
  699.8 18.3 %collective-permute-start.34 = (f32[3,258,1]{1,0,2:T(4,128)}, f32[3,258,1]{1,0,2:T(4,128)}, u32[]{:S(2)}, u32[]{:S(2)}) collective-permute-start(f32[3,258,1]{1,0,2:T(4,128)} %copy.696), channel_id=1, source_target_pairs={{1,0},{2,1},{3,2},{4,3},{5,4},{6,5},{7,6},{0,7},{9,8},{10,9},{11,1... | collective-permute-start | bytes 9296 | tf_op jit(solution)/shard_map/ppermute | solution.py:22
  709.5 10.4 collective-permute-start.3
  714.8 7.7 collective-permute-start.2
  751.4 9.3 collective-permute-start.39
  758.0 6.8 collective-permute-start.38
  770.8 6.8 collective-permute-start.41
  782.0 7.1 collective-permute-start.43
  808.8 7.3 collective-permute-start.47
  835.7 7.1 collective-permute-start.51
  862.6 7.3 collective-permute-start.55
  866.3 6.6 collective-permute-start.54
  891.5 7.2 collective-permute-start.59
  916.8 58.3 %collective-permute-start.61 = (f32[3,1,128]{2,0,1:T(4,128)}, f32[3,1,128]{2,0,1:T(4,128)}, u32[]{:S(2)}, u32[]{:S(2)}) collective-permute-start(f32[3,1,128]{2,0,1:T(4,128)} %get-tuple-element.263), channel_id=1, source_target_pairs={{8,0},{16,8},{24,16},{32,24},{40,32},{48,40},{56,48},{64,56},{72,6... | collective-permute-start | bytes 4616 | tf_op jit(solution)/shard_map/ppermute | solution.py:22
  922.2 52.9 %collective-permute-start.60 = (f32[3,1,128]{2,0,1:T(4,128)}, f32[3,1,128]{2,0,1:T(4,128)}, u32[]{:S(2)}, u32[]{:S(2)}) collective-permute-start(f32[3,1,128]{2,0,1:T(4,128)} %get-tuple-element.262), channel_id=1, source_target_pairs={{0,8},{8,16},{16,24},{24,32},{32,40},{40,48},{48,56},{56,64},{64,7... | collective-permute-start | bytes 4616 | tf_op jit(solution)/shard_map/ppermute | solution.py:19
  979.1 73.3 %collective-permute-start.63 = (f32[3,258,1]{1,0,2:T(4,128)}, f32[3,258,1]{1,0,2:T(4,128)}, u32[]{:S(2)}, u32[]{:S(2)}) collective-permute-start(f32[3,258,1]{1,0,2:T(4,128)} %copy.735), channel_id=1, source_target_pairs={{1,0},{2,1},{3,2},{4,3},{5,4},{6,5},{7,6},{0,7},{9,8},{10,9},{11,1... | collective-permute-start | bytes 9296 | tf_op jit(solution)/shard_map/ppermute | solution.py:22
  982.9 71.3 %collective-permute-start.62 = (f32[3,258,1]{1,0,2:T(4,128)}, f32[3,258,1]{1,0,2:T(4,128)}, u32[]{:S(2)}, u32[]{:S(2)}) collective-permute-start(f32[3,258,1]{1,0,2:T(4,128)} %copy.734), channel_id=1, source_target_pairs={{0,1},{1,2},{2,3},{3,4},{4,5},{5,6},{6,7},{7,0},{8,9},{9,10},{10,1... | collective-permute-start | bytes 9296 | tf_op jit(solution)/shard_map/ppermute | solution.py:19
  (138 other events, 1412.9 us)
where the time goes:
time: 1070 us; the launch traced here: 1060 us
  blocking collectives  510 us (48%)
  local copies, waits for them, and re-layouts  218 us (20%)
  starting transfers between devices  135 us (13%)
  other arithmetic  128 us (12%)
  loops' own time  47.1 us (4%)
  waiting for transfers between devices  19.6 us (2%)
    all_gather x1, blocking collectives, shards(): lax.all_gather(turbine_offset, ('gx', 'gy'), axis=0, tiled=True)  303 us
    unnamed x3, blocking collectives  207 us
    ppermute x32, starting transfers between devices, padded_2(): lax.ppermute(lax.slice_in_dim(block, 0, width, axis=dim), axis, backward)  116 us
    gather x36, local copies, waits for them, and re-layouts  49.5 us
    another operation x1, loops' own time, shards(): lax.fori_loop(0, slot_count, add_turbine, jnp.zeros_like(velocity))  47 us
    slice x37, local copies, waits for them, and re-layouts, padded_2(): lax.slice_in_dim(block, block.shape[dim] - width, None, axis=dim)  34.9 us
    sub x6, other arithmetic, advance(): center + advect * (upwind - center)  32.3 us
    slice x22, local copies, waits for them, and re-layouts, padded_2(): lax.slice_in_dim(block, 0, width, axis=dim)  25.5 us
  transfers between devices with their start and end apart: 64, of which 22 were waited for; matrix products, arithmetic and copies ran while one was open for 20% of the time, Pallas kernels for 0%

commit v1 on v0

--- a/solution.py
+++ b/solution.py
@@ -105,9 +105,16 @@
     velocity, adjoint_seed, courant, viscosity, turbine_tile, turbine_offset, thrust, disk_width
 ):
     levels = velocity.shape[0]
+
+    def perform_stocks(arr):
+        y1 = jnp.stack([arr for _ in range(jax.lax.axis_size(("gx", "gy")))])
+        w_next = jax.lax.all_to_all(y1, axis_name=("gx", "gy"), concat_axis=0, split_axis=0)
+        inter = jnp.concatenate(w_next, 0)
+        return inter
+
     places, shifts = (
         lax.all_gather(turbine_tile, ("gx", "gy"), axis=0, tiled=True),
-        lax.all_gather(turbine_offset, ("gx", "gy"), axis=0, tiled=True),
+        perform_stocks(turbine_offset),
     )
     thrusts, widths = (
         lax.all_gather(thrust, ("gx", "gy"), axis=0, tiled=True),

time: 1070 us -> 786 us (0.73)
  blocking collectives: 510 us -> 195 us
  local copies, waits for them, and re-layouts: 218 us -> 234 us
    all_gather x1 -> x0, blocking collectives: 303 us -> none  [shards(): lax.all_gather(turbine_offset, ('gx', 'gy'), axis=0, tiled=True)]
    dynamic_slice x24, local copies, waits for them, and re-layouts: 14.1 us -> 30.4 us  [add_turbine(): corner = (jnp.int32(0), slot_rows[slot_index], slot_cols[slot_index])]
    all_to_all x0 -> x1, starting transfers between devices: none -> 11.9 us  [perform_stocks(): jax.lax.all_to_all(y1, axis_name=('gx', 'gy'), concat_axis=0, split_axis=0)]
    unnamed x3, blocking collectives: 207 us -> 195 us
  transfers between devices with their start and end apart: 64 -> 65, of which waited for: 22 -> 19; matrix products, arithmetic and copies ran while one was open for 20% -> 30% of each run, Pallas kernels for 0% -> 0%
where the time goes in v1:
time: 786 us; the launch traced here: 773 us
  local copies, waits for them, and re-layouts  234 us (30%)
  blocking collectives  195 us (25%)
  starting transfers between devices  145 us (18%)
  other arithmetic  128 us (16%)
  loops' own time  50.1 us (6%)
  waiting for transfers between devices  18.6 us (2%)
    unnamed x3, blocking collectives  195 us
    ppermute x32, starting transfers between devices, padded_2(): lax.ppermute(lax.slice_in_dim(block, 0, width, axis=dim), axis, backward)  116 us
    another operation x1, loops' own time, shards(): lax.fori_loop(0, slot_count, add_turbine, jnp.zeros_like(velocity))  50 us
    gather x36, local copies, waits for them, and re-layouts  43.4 us
    slice x37, local copies, waits for them, and re-layouts, padded_2(): lax.slice_in_dim(block, block.shape[dim] - width, None, axis=dim)  32.8 us
    sub x6, other arithmetic, advance(): center + advect * (upwind - center)  32.4 us
    dynamic_slice x24, local copies, waits for them, and re-layouts, add_turbine(): corner = (jnp.int32(0), slot_rows[slot_index], slot_cols[slot_index])  30.4 us
    slice x22, local copies, waits for them, and re-layouts, padded_2(): lax.slice_in_dim(block, 0, width, axis=dim)  25.7 us
  transfers between devices with their start and end apart: 65, of which 19 were waited for; matrix products, arithmetic and copies ran while one was open for 30% of the time, Pallas kernels for 0%

profile of v1, /device:TPU:1, one launch (start us, length us, event | category | flops | bytes accessed | tf_op | source)
XLA Modules:
  0.0 773.5 jit_solution(12534742921013164514)
XLA Ops:
  5.5 11.9 %all-to-all-start = ((s32[128,4,2]{1,2,0:T(2,128)}), s32[128,4,2]{1,2,0:T(2,128)S(1)}, u32[]{:S(2)}, u32[]{:S(2)}) async-start(s32[128,4,2]{1,2,0:T(2,128)} %stack.2), calls=%async_computation | async-start | bytes 262144 | tf_op jit(solution)/shard_map/all_to_all | solution.py:111
  19.7 67.1 %all-reduce.32 = s32[512]{0:T(512)S(1)} all-reduce(s32[512]{0:T(512)S(1)} %bitcast_dynamic-update-slice_fusion.1), channel_id=1, replica_groups=mesh['gx'=16,'gy'=8] {'gx','gy'}, use_global_device_ids=true, to_apply=%add.32 | all-reduce | flops 512 | bytes 4096
  92.3 62.6 %all-reduce.36 = (f32[512]{0:T(512)S(1)}, f32[512]{0:T(512)S(1)}) all-reduce(f32[512]{0:T(512)S(1)} %dynamic-update-slice.3, f32[512]{0:T(512)S(1)} %dynamic-update-slice.4), channel_id=1, replica_groups=mesh['gx'=16,'gy'=8] {'gx','gy'}, use_global_device_ids=true, to_apply=%add.33 | all-reduce | flops 1024 | bytes 8192
  170.1 120.6 %while.14 = (s32[]{:T(128)}, f32[3,256,128]{2,1,0:T(8,128)S(1)}, s32[12]{0:T(128)}, s32[12]{0:T(128)}, f32[12]{0:T(128)S(1)}, /*index=5*/f32[12,3,64,64]{3,2,1,0...) while((s32[]{:T(128)}, f32[3,256,128]{2,1,0:T(8,128)S(1)}, s32[12]{0:T(128)}, s32[12]{0:T(128)}, ...), condition=%wide.region_2.3_spmd, body=%wide.region_1.2_spmd.sunk | while | flops 24584 | bytes 245993 | solution.py:144
  303.4 4.4 collective-permute-start.14
  310.1 6.0 fusion.113
  316.1 4.0 collective-permute-start.17
  327.4 4.0 collective-permute-start.18
  333.7 5.9 fusion.102
  350.5 4.4 collective-permute-start.22
  357.3 5.9 fusion.91
  363.3 5.2 collective-permute-start.25
  369.0 5.4 collective-permute-start.7
  377.6 5.1 collective-permute-start.26
  385.0 6.0 fusion.80
  398.3 5.4 collective-permute-start.30
  406.8 5.0 fusion.69
  423.0 5.1 collective-permute-start.34
  449.6 5.1 fusion.131
  454.8 4.9 fusion.130
  459.9 4.1 fusion.121
  464.0 5.7 collective-permute-start.37
  475.8 4.7 collective-permute-start.39
  495.2 6.0 collective-permute-start.41
  522.8 5.3 collective-permute-start.45
  551.1 5.2 collective-permute-start.49
  578.3 5.3 collective-permute-start.53
  605.8 4.9 collective-permute-start.57
  631.1 9.2 %multiply_subtract_fusion = (f32[3,256,128]{2,0,1:T(4,128)S(1)}, f32[3,256,128]{2,0,1:T(4,128)S(1)}) fusion(f32[3,256,128]{2,0,1:T(4,128)} %copy-done.41, f32[3,256,128]{2,0,1:T(4,128)S(1)} %copy-done.18, f32[3,256,128]{2,0,1:T(4,128)S(1)} %copy-done.15, f32[3,256,128]{2,0,1:T(4,128)S(1)} %copy-done.12, f32[3,256,128]{2,0,1:T(4,128)S(1)} %copy-done.9, ...), kind=kLoop, calls=%fused_computation.278 | loop fusion | flops 7766016 | bytes 11281456 | tf_op jit(solution)/shard_map/sub | solution.py:166
  642.0 5.2 collective-permute-start.61
  648.2 43.4 %while.15 = (s32[]{:T(128)}, f32[3,256,128]{2,1,0:T(8,128)}, s32[12,3]{0,1:T(4,128)S(1)}, f32[12,3,64,64]{3,2,1,0:T(8,128)}, s32[]{:T(128)}) while((s32[]{:T(128)}, f32[3,256,128]{2,1,0:T(8,128)}, s32[12,3]{0,1:T(4,128)S(1)}, f32[12,3,64,64]{3,2,1,0:T(8,128)}, s32[]{:T(128)}) %tuple.132), condition=%wide.while_cond, body=%wide.while_body.sunk | while | flops 2 | bytes 197749 | solution.py:188
  699.5 65.8 %all-reduce.35 = f32[512]{0:T(512)S(1)} all-reduce(f32[512]{0:T(512)S(1)} %select_reduce_fusion), channel_id=2, replica_groups=mesh['gx'=16,'gy'=8] {'gx','gy'}, use_global_device_ids=true, to_apply=%region_5.6.clone | all-reduce | flops 512 | bytes 4096
  (611 shorter events, 375.9 us)
Async XLA Ops:
  1.4 155.5 %collective-permute-start.9 = (f32[3,1,128]{2,1,0:T(1,128)S(1)}, f32[3,1,128]{2,1,0:T(1,128)S(1)}, u32[]{:S(2)}, u32[]{:S(2)}) collective-permute-start(f32[3,1,128]{2,1,0:T(1,128)S(1)} %get-tuple-element.326), channel_id=1, source_target_pairs={{8,0},{16,8},{24,16},{32,24},{40,32},{48,40},{56,48},{64,56},{72,6... | collective-permute-start | bytes 4616 | tf_op jit(solution)/shard_map/ppermute | solution.py:22
  2.8 154.1 %collective-permute-start.8 = (f32[3,1,128]{2,1,0:T(1,128)S(1)}, f32[3,1,128]{2,1,0:T(1,128)S(1)}, u32[]{:S(2)}, u32[]{:S(2)}) collective-permute-start(f32[3,1,128]{2,1,0:T(1,128)S(1)} %get-tuple-element.327), channel_id=1, source_target_pairs={{0,8},{8,16},{16,24},{24,32},{32,40},{40,48},{48,56},{56,64},{64,7... | collective-permute-start | bytes 4616 | tf_op jit(solution)/shard_map/ppermute | solution.py:19
  5.5 161.3 %all-to-all-start = ((s32[128,4,2]{1,2,0:T(2,128)}), s32[128,4,2]{1,2,0:T(2,128)S(1)}, u32[]{:S(2)}, u32[]{:S(2)}) async-start(s32[128,4,2]{1,2,0:T(2,128)} %stack.2), calls=%async_computation | async-start | bytes 262144 | tf_op jit(solution)/shard_map/all_to_all | solution.py:111
  159.9 130.8 %collective-permute-start.11 = (f32[3,258,1]{1,0,2:T(4,128)}, f32[3,258,1]{1,0,2:T(4,128)S(1)}, u32[]{:S(2)}, u32[]{:S(2)}) collective-permute-start(f32[3,258,1]{1,0,2:T(4,128)} %copy.745), channel_id=1, source_target_pairs={{0,1},{1,2},{2,3},{3,4},{4,5},{5,6},{6,7},{7,0},{8,9},{9,10},{10,1... | collective-permute-start | bytes 9296 | tf_op jit(solution)/shard_map/ppermute | solution.py:19
  162.5 129.3 %collective-permute-start.10 = (f32[3,258,1]{1,0,2:T(4,128)}, f32[3,258,1]{1,0,2:T(4,128)}, u32[]{:S(2)}, u32[]{:S(2)}) collective-permute-start(f32[3,258,1]{1,0,2:T(4,128)} %copy.744), channel_id=1, source_target_pairs={{1,0},{2,1},{3,2},{4,3},{5,4},{6,5},{7,6},{0,7},{9,8},{10,9},{11,1... | collective-permute-start | bytes 9296 | tf_op jit(solution)/shard_map/ppermute | solution.py:22
  316.1 6.9 collective-permute-start.17
  320.2 23.0 %collective-permute-start.5 = (f32[3,1,128]{2,1,0:T(1,128)S(1)}, f32[3,1,128]{2,1,0:T(1,128)S(1)}, u32[]{:S(2)}, u32[]{:S(2)}) collective-permute-start(f32[3,1,128]{2,1,0:T(1,128)S(1)} %get-tuple-element.329), channel_id=1, source_target_pairs={{8,0},{16,8},{24,16},{32,24},{40,32},{48,40},{56,48},{64,56},{72,6... | collective-permute-start | bytes 4616 | tf_op jit(solution)/shard_map/ppermute | solution.py:22
  320.8 23.0 %collective-permute-start.4 = (f32[3,1,128]{2,1,0:T(1,128)S(1)}, f32[3,1,128]{2,1,0:T(1,128)}, u32[]{:S(2)}, u32[]{:S(2)}) collective-permute-start(f32[3,1,128]{2,1,0:T(1,128)S(1)} %get-tuple-element.328), channel_id=1, source_target_pairs={{0,8},{8,16},{16,24},{24,32},{32,40},{40,48},{48,56},{56,64},{64,7... | collective-permute-start | bytes 4616 | tf_op jit(solution)/shard_map/ppermute | solution.py:19
  325.7 6.6 collective-permute-start.19
  349.1 6.7 collective-permute-start.23
  363.3 11.3 %collective-permute-start.25 = (f32[3,1,128]{2,0,1:T(4,128)S(1)}, f32[3,1,128]{2,0,1:T(4,128)S(1)}, u32[]{:S(2)}, u32[]{:S(2)}) collective-permute-start(f32[3,1,128]{2,0,1:T(4,128)S(1)} %get-tuple-element.299), channel_id=1, source_target_pairs={{8,0},{16,8},{24,16},{32,24},{40,32},{48,40},{56,48},{64,56},{72,6... | collective-permute-start | bytes 4616 | tf_op jit(solution)/shard_map/ppermute | solution.py:22
  369.0 26.0 %collective-permute-start.7 = (f32[3,258,1]{1,0,2:T(4,128)S(1)}, f32[3,258,1]{1,0,2:T(4,128)S(1)}, u32[]{:S(2)}, u32[]{:S(2)}) collective-permute-start(f32[3,258,1]{1,0,2:T(4,128)S(1)} %copy.741), channel_id=1, source_target_pairs={{1,0},{2,1},{3,2},{4,3},{5,4},{6,5},{7,6},{0,7},{9,8},{10,9},{11,1... | collective-permute-start | bytes 9296 | tf_op jit(solution)/shard_map/ppermute | solution.py:22
  374.6 21.6 %collective-permute-start.6 = (f32[3,258,1]{1,0,2:T(4,128)S(1)}, f32[3,258,1]{1,0,2:T(4,128)S(1)}, u32[]{:S(2)}, u32[]{:S(2)}) collective-permute-start(f32[3,258,1]{1,0,2:T(4,128)S(1)} %copy.740), channel_id=1, source_target_pairs={{0,1},{1,2},{2,3},{3,4},{4,5},{5,6},{6,7},{7,0},{8,9},{9,10},{10,1... | collective-permute-start | bytes 9296 | tf_op jit(solution)/shard_map/ppermute | solution.py:19
  398.3 7.4 collective-permute-start.30
  415.2 12.9 %collective-permute-start.1 = (f32[9,1,128]{2,0,1:T(8,128)S(1)}, f32[9,1,128]{2,0,1:T(8,128)S(1)}, u32[]{:S(2)}, u32[]{:S(2)}) collective-permute-start(f32[9,1,128]{2,0,1:T(8,128)S(1)} %get-tuple-element.233), channel_id=1, source_target_pairs={{8,0},{16,8},{24,16},{32,24},{40,32},{48,40},{56,48},{64,56},{72,6... | collective-permute-start | bytes 13832 | tf_op jit(solution)/shard_map/ppermute | solution.py:22
  417.2 10.9 %collective-permute-start = (f32[9,1,128]{2,0,1:T(8,128)S(1)}, f32[9,1,128]{2,0,1:T(8,128)S(1)}, u32[]{:S(2)}, u32[]{:S(2)}) collective-permute-start(f32[9,1,128]{2,0,1:T(8,128)S(1)} %get-tuple-element.232), channel_id=1, source_target_pairs={{0,8},{8,16},{16,24},{24,32},{32,40},{40,48},{48,56},{56,64},{64,7... | collective-permute-start | bytes 13832 | tf_op jit(solution)/shard_map/ppermute | solution.py:19
  421.1 19.7 %collective-permute-start.35 = (f32[3,258,1]{1,0,2:T(4,128)S(1)}, f32[3,258,1]{1,0,2:T(4,128)}, u32[]{:S(2)}, u32[]{:S(2)}) collective-permute-start(f32[3,258,1]{1,0,2:T(4,128)S(1)} %copy.696), channel_id=1, source_target_pairs={{0,1},{1,2},{2,3},{3,4},{4,5},{5,6},{6,7},{7,0},{8,9},{9,10},{10,1... | collective-permute-start | bytes 9296 | tf_op jit(solution)/shard_map/ppermute | solution.py:19
  423.0 19.5 %collective-permute-start.34 = (f32[3,258,1]{1,0,2:T(4,128)}, f32[3,258,1]{1,0,2:T(4,128)}, u32[]{:S(2)}, u32[]{:S(2)}) collective-permute-start(f32[3,258,1]{1,0,2:T(4,128)} %copy.694), channel_id=1, source_target_pairs={{1,0},{2,1},{3,2},{4,3},{5,4},{6,5},{7,6},{0,7},{9,8},{10,9},{11,1... | collective-permute-start | bytes 9296 | tf_op jit(solution)/shard_map/ppermute | solution.py:22
  434.0 10.4 %collective-permute-start.3 = (f32[9,258,1]{1,0,2:T(8,128)S(1)}, f32[9,258,1]{1,0,2:T(8,128)S(1)}, u32[]{:S(2)}, u32[]{:S(2)}) collective-permute-start(f32[9,258,1]{1,0,2:T(8,128)S(1)} %copy.628), channel_id=1, source_target_pairs={{1,0},{2,1},{3,2},{4,3},{5,4},{6,5},{7,6},{0,7},{9,8},{10,9},{11,1... | collective-permute-start | bytes 27872 | tf_op jit(solution)/shard_map/ppermute | solution.py:22
  439.2 7.8 %collective-permute-start.2 = (f32[9,258,1]{1,0,2:T(8,128)S(1)}, f32[9,258,1]{1,0,2:T(8,128)S(1)}, u32[]{:S(2)}, u32[]{:S(2)}) collective-permute-start(f32[9,258,1]{1,0,2:T(8,128)S(1)} %copy.627), channel_id=1, source_target_pairs={{0,1},{1,2},{2,3},{3,4},{4,5},{5,6},{6,7},{7,0},{8,9},{9,10},{10,1... | collective-permute-start | bytes 27872 | tf_op jit(solution)/shard_map/ppermute | solution.py:19
  475.8 9.3 %collective-permute-start.39 = (f32[3,258,1]{1,0,2:T(4,128)}, f32[3,258,1]{1,0,2:T(4,128)}, u32[]{:S(2)}, u32[]{:S(2)}) collective-permute-start(f32[3,258,1]{1,0,2:T(4,128)} %copy.703), channel_id=1, source_target_pairs={{1,0},{2,1},{3,2},{4,3},{5,4},{6,5},{7,6},{0,7},{9,8},{10,9},{11,1... | collective-permute-start | bytes 9296 | tf_op jit(solution)/shard_map/ppermute | solution.py:22
  482.4 6.8 collective-permute-start.38
  495.2 6.8 collective-permute-start.41
  506.5 7.1 collective-permute-start.43
  533.4 7.3 collective-permute-start.47
  562.1 7.1 collective-permute-start.51
  589.3 7.3 collective-permute-start.55
  616.1 7.2 collective-permute-start.59
  642.0 51.5 %collective-permute-start.61 = (f32[3,1,128]{2,0,1:T(4,128)S(1)}, f32[3,1,128]{2,0,1:T(4,128)S(1)}, u32[]{:S(2)}, u32[]{:S(2)}) collective-permute-start(f32[3,1,128]{2,0,1:T(4,128)S(1)} %get-tuple-element.263), channel_id=1, source_target_pairs={{8,0},{16,8},{24,16},{32,24},{40,32},{48,40},{56,48},{64,56},{72,6... | collective-permute-start | bytes 4616 | tf_op jit(solution)/shard_map/ppermute | solution.py:22
  647.2 46.3 %collective-permute-start.60 = (f32[3,1,128]{2,0,1:T(4,128)S(1)}, f32[3,1,128]{2,0,1:T(4,128)S(1)}, u32[]{:S(2)}, u32[]{:S(2)}) collective-permute-start(f32[3,1,128]{2,0,1:T(4,128)S(1)} %get-tuple-element.262), channel_id=1, source_target_pairs={{0,8},{8,16},{16,24},{24,32},{32,40},{40,48},{48,56},{56,64},{64,7... | collective-permute-start | bytes 4616 | tf_op jit(solution)/shard_map/ppermute | solution.py:19
  696.1 69.8 %collective-permute-start.63 = (f32[3,258,1]{1,0,2:T(4,128)S(1)}, f32[3,258,1]{1,0,2:T(4,128)S(1)}, u32[]{:S(2)}, u32[]{:S(2)}) collective-permute-start(f32[3,258,1]{1,0,2:T(4,128)S(1)} %copy.733), channel_id=1, source_target_pairs={{1,0},{2,1},{3,2},{4,3},{5,4},{6,5},{7,6},{0,7},{9,8},{10,9},{11,1... | collective-permute-start | bytes 9296 | tf_op jit(solution)/shard_map/ppermute | solution.py:22
  698.3 68.6 %collective-permute-start.62 = (f32[3,258,1]{1,0,2:T(4,128)S(1)}, f32[3,258,1]{1,0,2:T(4,128)S(1)}, u32[]{:S(2)}, u32[]{:S(2)}) collective-permute-start(f32[3,258,1]{1,0,2:T(4,128)S(1)} %copy.732), channel_id=1, source_target_pairs={{0,1},{1,2},{2,3},{3,4},{4,5},{5,6},{6,7},{7,0},{8,9},{9,10},{10,1... | collective-permute-start | bytes 9296 | tf_op jit(solution)/shard_map/ppermute | solution.py:19
  (143 other events, 1137.6 us)
